TPU v7x, 32 devices: a whole 2x2x4 slice. The times are simulated.
32 devices in a mesh: ctx: 8 (over z, x), fsdp: 4 (over y, core).
Axes of the slice: x: 2, y: 2, z: 4, core: 2. Of those that a mesh axis runs over, the one named last changes fastest.
Arguments:
- tokens: bfloat16 [4, 1024, 1536], P('fsdp', 'ctx'), may hold values from -6 to 6
- segments: int32 [4, 1024], P('fsdp'), may hold values from 0 to 3, never falling along the last dimension, each value on 1 to 512 neighbouring positions
- gain_attn: bfloat16 [1536], replicated, may hold values from 0.5 to 1.5
- w_query: bfloat16 [1536, 1536], P('fsdp'), may hold values from -0.15625 to 0.15625
- w_key: bfloat16 [1536, 1536], P('fsdp'), may hold values from -0.15625 to 0.15625
- w_value: bfloat16 [1536, 1536], P('fsdp'), may hold values from -0.15625 to 0.15625
- w_forget: bfloat16 [1536, 24], P('fsdp'), may hold values from -0.15625 to 0.15625
- forget_bias: float32 [24], replicated, may hold values from 2 to 8
- w_outgate: bfloat16 [1536, 1536], P('fsdp'), may hold values from -0.15625 to 0.15625
- w_out: bfloat16 [1536, 1536], P('fsdp'), may hold values from -0.625 to 0.625
- gain_ffn: bfloat16 [1536], replicated, may hold values from 0.5 to 1.5
- w_gate: bfloat16 [1536, 4096], P('fsdp'), may hold values from -0.15625 to 0.15625
- w_up: bfloat16 [1536, 4096], P('fsdp'), may hold values from -0.15625 to 0.15625
- w_down: bfloat16 [4096, 1536], P('fsdp'), may hold values from -0.09375 to 0.09375
- cotangent: bfloat16 [4, 1024, 1536], P('fsdp', 'ctx'), may hold values from -6 to 6
Outputs:
- output: bfloat16 [4, 1024, 1536], P('fsdp', 'ctx')
- grad_tokens: float32 [4, 1024, 1536], P('fsdp', 'ctx')
- grad_gain_attn: float32 [1536], replicated
- grad_query: float32 [1536, 1536], P('fsdp')
- grad_key: float32 [1536, 1536], P('fsdp')
- grad_value: float32 [1536, 1536], P('fsdp')
- grad_forget: float32 [1536, 24], P('fsdp')
- grad_bias: float32 [24], replicated
- grad_outgate: float32 [1536, 1536], P('fsdp')
- grad_out: float32 [1536, 1536], P('fsdp')
- grad_gain_ffn: float32 [1536], replicated
- grad_gate: float32 [1536, 4096], P('fsdp')
- grad_up: float32 [1536, 4096], P('fsdp')
- grad_down: float32 [4096, 1536], P('fsdp')
Inputs may be any that keep to these rules, and one draw needn't show every extreme that they name: `segments`: along each sequence the document numbers never fall; every document has 1 to 512 tokens and one has exactly 512.
All inputs are finite; a program needn't handle non-finite values.
Results may differ from a plain program's by a relative error of at most 0.014.
Values may be sent and summed in bfloat16 or wider, within the bound.
A program may use at most 448 MiB of HBM per device.

v0:
```python
import math
import jax
import jax.numpy as jnp
from jax import lax
from jax.sharding import PartitionSpec as P

EPSILON = 1e-06
NEGATIVE = -1e30


def entering(value, axis, join, neutral, backward):
    count, mine = (lax.axis_size(axis), lax.axis_index(axis))
    pieces = lax.all_gather(value, axis)
    if backward:
        pieces = pieces[::-1]
        mine = count - 1 - mine
    subtotal = jnp.full_like(value, 0) + jnp.asarray(neutral, value.dtype)

    def hop(position, subtotal):
        longer = join(subtotal, pieces[position])
        return jnp.where(position < mine, longer, subtotal)

    return lax.fori_loop(0, count - 1, hop, subtotal)


def matmul(left, right):
    return jnp.dot(left, right, preferred_element_type=jnp.float32)


def matmul_rows(left, right):
    return lax.dot_general(
        left, right, (((1,), (1,)), ((), ())), preferred_element_type=jnp.float32
    )


def weight_grad(left, right):
    return lax.dot_general(
        left, right, (((0,), (0,)), ((), ())), preferred_element_type=jnp.float32
    )


def rms_stats(values):
    rstat = lax.rsqrt(jnp.mean(values * values, axis=-1, keepdims=True) + EPSILON)
    return (values * rstat, rstat)


def norm_back(grad_in, normed, rstat, gain):
    grad_normed = grad_in * gain
    grad_gain = jnp.sum(grad_in * normed, axis=0)
    grad_values = rstat * (
        grad_normed - normed * jnp.mean(grad_normed * normed, axis=-1, keepdims=True)
    )
    return (grad_values, grad_gain)


def shards(
    tokens,
    segments,
    gain_attn,
    w_query,
    w_key,
    w_value,
    w_forget,
    forget_bias,
    w_outgate,
    w_out,
    gain_ffn,
    w_gate,
    w_up,
    w_down,
    cotangent,
):
    gathered = (
        lax.all_gather(w_query, "fsdp", axis=0, tiled=True),
        lax.all_gather(w_key, "fsdp", axis=0, tiled=True),
        lax.all_gather(w_value, "fsdp", axis=0, tiled=True),
        lax.all_gather(w_forget, "fsdp", axis=0, tiled=True),
        lax.all_gather(w_outgate, "fsdp", axis=0, tiled=True),
        lax.all_gather(w_out, "fsdp", axis=0, tiled=True),
        lax.all_gather(w_gate, "fsdp", axis=0, tiled=True),
        lax.all_gather(w_up, "fsdp", axis=0, tiled=True),
        lax.all_gather(w_down, "fsdp", axis=0, tiled=True),
    )
    (
        full_query,
        full_key,
        full_value,
        full_forget,
        full_outgate,
        full_out,
        full_gate,
        full_up,
        full_down,
    ) = gathered
    inputs = tokens[0].astype(jnp.float32)
    tok_rows = inputs.shape[0]
    model_width = inputs.shape[1]
    n_heads = forget_bias.shape[0]
    head_dim = model_width // n_heads
    per_group = math.gcd(n_heads, 2)
    n_groups = n_heads // per_group
    group_width = per_group * head_dim
    scaling = head_dim ** (-0.5)
    n_ctx = lax.axis_size("ctx")
    position = lax.axis_index("ctx")
    seq_rows = tok_rows * n_ctx
    seg_all = segments[0]
    first_row = position * tok_rows
    pos_here = first_row + jnp.arange(tok_rows, dtype=jnp.int32)
    seg_here = lax.dynamic_slice_in_dim(seg_all, first_row, tok_rows, 0)
    pos_all = jnp.arange(seq_rows, dtype=jnp.int32)
    allowed = (pos_all[None, :] <= pos_here[:, None]) & (seg_all[None, :] == seg_here[:, None])
    gain_one = gain_attn.astype(jnp.float32)
    normed_one, rstat_one = rms_stats(inputs)
    normed = (normed_one * gain_one).astype(jnp.bfloat16)
    queries = matmul(normed, full_query).astype(jnp.bfloat16)
    key_own = matmul(normed, full_key).astype(jnp.bfloat16)
    value_own = matmul(normed, full_value).astype(jnp.bfloat16)
    forget_logits = matmul(normed, full_forget) + forget_bias
    log_keep = jax.nn.log_sigmoid(forget_logits)
    before = entering(
        jnp.sum(log_keep, axis=0), "ctx", jnp.add, jnp.zeros((n_heads,), jnp.float32), False
    )
    sent_rows = before[None, :] + jnp.cumsum(log_keep, axis=0)
    arrived = lax.all_gather(sent_rows, "ctx", axis=0, tiled=True)
    keys_all, values_all = (
        lax.all_gather(key_own, "ctx", axis=0, tiled=True),
        lax.all_gather(value_own, "ctx", axis=0, tiled=True),
    )

    def group_slices(group_index):
        column = group_index * group_width
        query_part = lax.dynamic_slice_in_dim(queries, column, group_width, 1).reshape(
            tok_rows, per_group, head_dim
        )
        key_part = lax.dynamic_slice_in_dim(keys_all, column, group_width, 1).reshape(
            seq_rows, per_group, head_dim
        )
        value_part = lax.dynamic_slice_in_dim(values_all, column, group_width, 1).reshape(
            seq_rows, per_group, head_dim
        )
        decay_rows = lax.dynamic_slice_in_dim(sent_rows, group_index * per_group, per_group, 1)
        decay_keys = lax.dynamic_slice_in_dim(arrived, group_index * per_group, per_group, 1)
        scores = (
            jnp.einsum("bhd,nhd->hbn", query_part, key_part, preferred_element_type=jnp.float32)
            * scaling
        )
        scores = scores + decay_rows.T[:, :, None] - decay_keys.T[:, None, :]
        scores = jnp.where(allowed[None], scores, NEGATIVE)
        return (query_part, key_part, value_part, scores)

    def forward_group(group_index):
        query_part, key_part, value_part, scores = group_slices(group_index)
        row_max = jnp.max(scores, axis=-1, keepdims=True)
        raised = jnp.exp(scores - row_max)
        row_total = jnp.sum(raised, axis=-1, keepdims=True)
        probabilities = raised / row_total
        mixed_part = jnp.einsum(
            "hbn,nhd->bhd",
            probabilities.astype(jnp.bfloat16),
            value_part,
            preferred_element_type=jnp.float32,
        )
        return (mixed_part.reshape(tok_rows, group_width), (row_max + jnp.log(row_total))[:, :, 0])

    mixed_groups, log_totals = lax.map(forward_group, jnp.arange(n_groups, dtype=jnp.int32))
    attended = jnp.moveaxis(mixed_groups, 0, 1).reshape(tok_rows, model_width)
    gate_logits = matmul(normed, full_outgate)
    gate_value = jax.nn.sigmoid(gate_logits)
    gated_out = (attended * gate_value).astype(jnp.bfloat16)
    middle = inputs + matmul(gated_out, full_out)
    gain_two = gain_ffn.astype(jnp.float32)
    normed_two_f, rstat_two = rms_stats(middle)
    normed_two = (normed_two_f * gain_two).astype(jnp.bfloat16)
    gate_part = matmul(normed_two, full_gate)
    up_part = matmul(normed_two, full_up)
    sig_gate = jax.nn.sigmoid(gate_part)
    silu_gate = gate_part * sig_gate
    hidden = (silu_gate * up_part).astype(jnp.bfloat16)
    output = middle + matmul(hidden, full_down)
    grad_out_low = cotangent[0]
    grad_output = grad_out_low.astype(jnp.float32)
    grad_hidden = matmul_rows(grad_out_low, full_down)
    grad_gate_low = (
        grad_hidden * up_part * (sig_gate * (1.0 + gate_part * (1.0 - sig_gate)))
    ).astype(jnp.bfloat16)
    grad_up_low = (grad_hidden * silu_gate).astype(jnp.bfloat16)
    grad_normed_two = matmul_rows(grad_gate_low, full_gate) + matmul_rows(grad_up_low, full_up)
    back_two, grad_gain_two = norm_back(grad_normed_two, normed_two_f, rstat_two, gain_two)
    grad_middle = grad_output + back_two
    ffn_parts = (
        lax.psum_scatter(
            weight_grad(normed_two, grad_gate_low), "fsdp", scatter_dimension=0, tiled=True
        ),
        lax.psum_scatter(
            weight_grad(normed_two, grad_up_low), "fsdp", scatter_dimension=0, tiled=True
        ),
        lax.psum_scatter(
            weight_grad(hidden, grad_out_low), "fsdp", scatter_dimension=0, tiled=True
        ),
    )
    grad_branch_low = grad_middle.astype(jnp.bfloat16)
    grad_gated = matmul_rows(grad_branch_low, full_out)
    grad_attn_low = (grad_gated * gate_value).astype(jnp.bfloat16)
    grad_gatelog_low = (grad_gated * attended * (gate_value * (1.0 - gate_value))).astype(
        jnp.bfloat16
    )

    def backward_group(group_index, carried):
        grad_queries, grad_keys, grad_values, grad_rowdecay, grad_keydecay = carried
        query_part, key_part, value_part, scores = group_slices(group_index)
        probabilities = jnp.exp(scores - log_totals[group_index][:, :, None])
        column = group_index * group_width
        grad_part = lax.dynamic_slice_in_dim(grad_attn_low, column, group_width, 1).reshape(
            tok_rows, per_group, head_dim
        )
        grad_vpart = jnp.einsum(
            "hbn,bhd->nhd",
            probabilities.astype(jnp.bfloat16),
            grad_part,
            preferred_element_type=jnp.float32,
        )
        grad_probs = jnp.einsum(
            "bhd,nhd->hbn", grad_part, value_part, preferred_element_type=jnp.float32
        )
        row_inner = jnp.sum(probabilities * grad_probs, axis=-1, keepdims=True)
        grad_scores = (probabilities * (grad_probs - row_inner)).astype(jnp.bfloat16)
        grad_qpart = (
            jnp.einsum("hbn,nhd->bhd", grad_scores, key_part, preferred_element_type=jnp.float32)
            * scaling
        )
        grad_kpart = (
            jnp.einsum("hbn,bhd->nhd", grad_scores, query_part, preferred_element_type=jnp.float32)
            * scaling
        )
        score_sums = grad_scores.astype(jnp.float32)
        grad_queries = lax.dynamic_update_slice_in_dim(
            grad_queries, grad_qpart.reshape(tok_rows, group_width), column, 1
        )
        grad_keys = lax.dynamic_update_slice_in_dim(
            grad_keys, grad_kpart.reshape(seq_rows, group_width), column, 1
        )
        grad_values = lax.dynamic_update_slice_in_dim(
            grad_values, grad_vpart.reshape(seq_rows, group_width), column, 1
        )
        grad_rowdecay = lax.dynamic_update_slice_in_dim(
            grad_rowdecay, jnp.sum(score_sums, axis=-1).T, group_index * per_group, 1
        )
        grad_keydecay = lax.dynamic_update_slice_in_dim(
            grad_keydecay, -jnp.sum(score_sums, axis=1).T, group_index * per_group, 1
        )
        return (grad_queries, grad_keys, grad_values, grad_rowdecay, grad_keydecay)

    initial = (
        jnp.zeros((tok_rows, model_width), jnp.float32),
        jnp.zeros((seq_rows, model_width), jnp.float32),
        jnp.zeros((seq_rows, model_width), jnp.float32),
        jnp.zeros((tok_rows, n_heads), jnp.float32),
        jnp.zeros((seq_rows, n_heads), jnp.float32),
    )
    grad_queries, grad_keys, grad_values, grad_rowdecay, grad_keydecay = lax.fori_loop(
        0, n_groups, backward_group, initial
    )
    key_back = (
        lax.psum_scatter(grad_keys, "ctx", scatter_dimension=0, tiled=True),
        lax.psum_scatter(grad_values, "ctx", scatter_dimension=0, tiled=True),
        lax.psum_scatter(grad_keydecay, "ctx", scatter_dimension=0, tiled=True),
    )
    grad_query_low = grad_queries.astype(jnp.bfloat16)
    grad_key_low = key_back[0].astype(jnp.bfloat16)
    grad_value_low = key_back[1].astype(jnp.bfloat16)
    decay_grad = grad_rowdecay + key_back[2]
    local_suffix = jnp.flip(jnp.cumsum(jnp.flip(decay_grad, 0), axis=0), 0)
    block_total = jnp.sum(decay_grad, axis=0)
    later_sum = entering(block_total, "ctx", jnp.add, jnp.zeros((n_heads,), jnp.float32), True)
    grad_logits_low = ((local_suffix + later_sum[None, :]) * jax.nn.sigmoid(-forget_logits)).astype(
        jnp.bfloat16
    )
    grad_bias = jnp.sum(grad_logits_low.astype(jnp.float32), axis=0)
    grad_normed = (
        matmul_rows(grad_query_low, full_query)
        + matmul_rows(grad_key_low, full_key)
        + matmul_rows(grad_value_low, full_value)
        + matmul_rows(grad_logits_low, full_forget)
        + matmul_rows(grad_gatelog_low, full_outgate)
    )
    back_one, grad_gain_one = norm_back(grad_normed, normed_one, rstat_one, gain_one)
    grad_inputs = grad_middle + back_one
    attn_parts = (
        lax.psum_scatter(
            weight_grad(normed, grad_query_low), "fsdp", scatter_dimension=0, tiled=True
        ),
        lax.psum_scatter(
            weight_grad(normed, grad_key_low), "fsdp", scatter_dimension=0, tiled=True
        ),
        lax.psum_scatter(
            weight_grad(normed, grad_value_low), "fsdp", scatter_dimension=0, tiled=True
        ),
        lax.psum_scatter(
            weight_grad(normed, grad_logits_low), "fsdp", scatter_dimension=0, tiled=True
        ),
        lax.psum_scatter(
            weight_grad(normed, grad_gatelog_low), "fsdp", scatter_dimension=0, tiled=True
        ),
        lax.psum_scatter(
            weight_grad(gated_out, grad_branch_low), "fsdp", scatter_dimension=0, tiled=True
        ),
    )
    summed = lax.psum(
        (
            ffn_parts[0],
            ffn_parts[1],
            ffn_parts[2],
            attn_parts[0],
            attn_parts[1],
            attn_parts[2],
            attn_parts[3],
            attn_parts[4],
            attn_parts[5],
        ),
        "ctx",
    )
    small_grads = lax.psum((grad_gain_one, grad_gain_two, grad_bias), ("ctx", "fsdp"))
    return (
        output.astype(jnp.bfloat16)[None],
        grad_inputs[None],
        small_grads[0],
        summed[3],
        summed[4],
        summed[5],
        summed[6],
        small_grads[2],
        summed[7],
        summed[8],
        small_grads[1],
        summed[0],
        summed[1],
        summed[2],
    )


def solution(mesh):
    return jax.shard_map(
        shards,
        mesh=mesh,
        in_specs=(
            P("fsdp", "ctx", None),
            P("fsdp", None),
            P(),
            P("fsdp", None),
            P("fsdp", None),
            P("fsdp", None),
            P("fsdp", None),
            P(),
            P("fsdp", None),
            P("fsdp", None),
            P(),
            P("fsdp", None),
            P("fsdp", None),
            P("fsdp", None),
            P("fsdp", "ctx", None),
        ),
        out_specs=(
            P("fsdp", "ctx", None),
            P("fsdp", "ctx", None),
            P(),
            P("fsdp", None),
            P("fsdp", None),
            P("fsdp", None),
            P("fsdp", None),
            P(),
            P("fsdp", None),
            P("fsdp", None),
            P(),
            P("fsdp", None),
            P("fsdp", None),
            P("fsdp", None),
        ),
        check_vma=False,
    )
```

profile of v0, /device:TPU:0, one launch (start us, length us, event | category | flops | bytes accessed | tf_op | source)
XLA Modules:
  0.0 2965.8 jit_solution(18028929066030934375)
XLA Ops:
  11.3 38.5 %all-gather.13.cloned.1.call-done = bf16[1536,1536]{1,0:T(8,128)(2,1)} async-done(((bf16[384,1536]{1,0:T(8,128)(2,1)}), bf16[1536,1536]{1,0:T(8,128)(2,1)}) %all-gather.13.cloned.1.call-update) | async-done | bytes 4718608 | tf_op jit(solution)/shard_map/all_gather | solution.py:76
  49.8 4.0 convolution_convert_fusion.2
  53.9 34.9 %all-gather.19.cloned.1.call-done = bf16[1536,1536]{1,0:T(8,128)(2,1)} async-done(((bf16[384,1536]{1,0:T(8,128)(2,1)}), bf16[1536,1536]{1,0:T(8,128)(2,1)}) %all-gather.19.cloned.1.call-update) | async-done | bytes 4718608 | tf_op jit(solution)/shard_map/all_gather | solution.py:75
  88.8 3.9 convolution_convert_fusion
  96.3 5.3 all_gather.51
  104.7 21.3 all-reduce
  127.3 32.3 %all_gather.53 = f32[1024,24]{1,0:T(8,128)S(1)} all-gather(f32[128,24]{1,0:T(8,128)S(1)} %broadcast_add_fusion), channel_id=1, replica_groups=mesh['ctx'=8,'fsdp'=4] {'ctx'}, dimensions={0}, use_global_device_ids=true | all-gather | bytes 110592 | tf_op jit(solution)/shard_map/all_gather | solution.py:125
  162.1 3.2 convolution_convert_fusion.1
  166.2 26.5 all-gather.15.cloned.1.call-done
  192.7 3.2 copy.45
  195.9 58.5 %all-gather.21.cloned.1.call-done = bf16[1024,1536]{1,0:T(8,128)(2,1)} async-done(((bf16[128,1536]{1,0:T(8,128)(2,1)}), bf16[1024,1536]{1,0:T(8,128)(2,1)}) %all-gather.21.cloned.1.call-update) | async-done | bytes 3145744 | tf_op jit(solution)/shard_map/all_gather | solution.py:127
  254.4 4.6 copy.47
  259.6 142.4 %while.63 = (s32[]{:T(128)}, f32[12,128,128]{1,2,0:T(8,128)}, f32[12,2,128]{2,1,0:T(2,128)}, s32[12]{0:T(128)}, bf16[1024,1536]{0,1:T(8,128)(2,1)S(1)}, /*index=...) while((s32[]{:T(128)}, f32[12,128,128]{1,2,0:T(8,128)}, ...), condition=%wide.region_8.9_spmd.clone, body=%wide.region_5.8_spmd.clone.sunk | while | flops 70123272 | bytes 5316909 | solution.py:166
  261.5 1.8 constant_dynamic-slice_fusion.16
  320.6 1.8 constant_dynamic-slice_fusion.16
  344.3 1.8 constant_dynamic-slice_fusion.16
  379.8 1.8 constant_dynamic-slice_fusion.16
  402.0 2.9 copy.50
  404.9 4.7 multiply_convert_fusion.6
  409.5 3.4 multiply_reduce_fusion.3
  414.8 7.7 fusion.77
  422.5 76.0 %all-gather.29.cloned.1.call-done = bf16[1536,4096]{1,0:T(8,128)(2,1)} async-done(((bf16[384,4096]{1,0:T(8,128)(2,1)}), bf16[1536,4096]{1,0:T(8,128)(2,1)}) %all-gather.29.cloned.1.call-update) | async-done | bytes 12582928 | tf_op jit(solution)/shard_map/all_gather | solution.py:81
  498.5 7.7 fusion.78
  506.2 75.9 %all-gather.31.cloned.1.call-done = bf16[4096,1536]{1,0:T(8,128)(2,1)} async-done(((bf16[1024,1536]{1,0:T(8,128)(2,1)}), bf16[4096,1536]{1,0:T(8,128)(2,1)}) %all-gather.31.cloned.1.call-update) | async-done | bytes 12582928 | tf_op jit(solution)/shard_map/all_gather | solution.py:82
  582.1 11.7 multiply_convert_fusion.1
  593.8 10.2 fusion.79
  604.0 7.4 multiply_reduce_fusion.1
  612.8 5.5 multiply_convert_fusion.4
  619.1 3.5 broadcast.106
  622.6 3.5 broadcast.106.clone
  626.1 118.0 %while.64 = (s32[]{:T(128)}, bf16[128,1536]{0,1:T(8,128)(2,1)}, f32[1024,1536]{0,1:T(8,128)}, f32[1024,1536]{0,1:T(8,128)}, f32[128,24]{0,1:T(8,128)S(1)}, /*ind...) while((s32[]{:T(128)}, bf16[128,1536]{0,1:T(8,128)(2,1)}, ...), condition=%wide.region_15.16_spmd.clone, body=%wide.region_11.15_spmd.clone.sunk | while | flops 171998720 | bytes 13599061 | solution.py:261
  745.6 5.2 fusion.52
  750.8 5.0 fusion.62
  757.0 6.0 fusion.56
  763.0 99.6 %reduce-scatter.13.cloned.1.call-done = f32[128,1536]{0,1:T(8,128)} async-done(((f32[1024,1536]{0,1:T(8,128)}), f32[128,1536]{0,1:T(8,128)}) %reduce-scatter.13.cloned.1.call-update) | async-done | bytes 786448 | tf_op jit(solution)/shard_map/reduce_scatter | solution.py:265
  862.6 6.2 fusion.49
  869.1 115.0 %reduce-scatter.15.cloned.1.call-done = f32[128,1536]{0,1:T(8,128)} async-done(((f32[1024,1536]{0,1:T(8,128)}), f32[128,1536]{0,1:T(8,128)}) %reduce-scatter.15.cloned.1.call-update) | async-done | bytes 786448 | tf_op jit(solution)/shard_map/reduce_scatter | solution.py:266
  984.2 6.2 fusion.46
  990.4 11.4 fusion.81
  1001.9 11.4 fusion.82
  1014.2 11.5 fusion.42
  1025.8 19.3 reduce-scatter.17.cloned.1.call-done
  1046.7 19.5 all-reduce.1
  1067.8 57.4 %reduce-scatter.19.cloned.1.call-done = f32[384,1536]{1,0:T(8,128)} async-done(((f32[1536,1536]{1,0:T(8,128)}), f32[384,1536]{1,0:T(8,128)}) %reduce-scatter.19.cloned.1.call-update) | async-done | bytes 2359312 | tf_op jit(solution)/shard_map/reduce_scatter | solution.py:290
  1125.1 80.9 %reduce-scatter.27.cloned.1.call-done = f32[384,1536]{1,0:T(8,128)} async-done(((f32[1536,1536]{1,0:T(8,128)}), f32[384,1536]{1,0:T(8,128)}) %reduce-scatter.27.cloned.1.call-update) | async-done | bytes 2359312 | tf_op jit(solution)/shard_map/reduce_scatter | solution.py:302
  1206.0 80.9 %reduce-scatter.29.cloned.1.call-done = f32[384,1536]{1,0:T(8,128)} async-done(((f32[1536,1536]{1,0:T(8,128)}), f32[384,1536]{1,0:T(8,128)}) %reduce-scatter.29.cloned.1.call-update) | async-done | bytes 2359312 | tf_op jit(solution)/shard_map/reduce_scatter | solution.py:305
  1286.9 80.9 %reduce-scatter.21.cloned.1.call-done = f32[384,1536]{1,0:T(8,128)} async-done(((f32[1536,1536]{1,0:T(8,128)}), f32[384,1536]{1,0:T(8,128)}) %reduce-scatter.21.cloned.1.call-update) | async-done | bytes 2359312 | tf_op jit(solution)/shard_map/reduce_scatter | solution.py:293
  1367.8 80.9 %reduce-scatter.23.cloned.1.call-done = f32[384,1536]{1,0:T(8,128)} async-done(((f32[1536,1536]{1,0:T(8,128)}), f32[384,1536]{1,0:T(8,128)}) %reduce-scatter.23.cloned.1.call-update) | async-done | bytes 2359312 | tf_op jit(solution)/shard_map/reduce_scatter | solution.py:296
  1448.8 183.1 %reduce-scatter.31.cloned.1.call-done = f32[384,4096]{1,0:T(8,128)} async-done(((f32[1536,4096]{1,0:T(8,128)}), f32[384,4096]{1,0:T(8,128)}) %reduce-scatter.31.cloned.1.call-update) | async-done | bytes 6291472 | tf_op jit(solution)/shard_map/reduce_scatter | solution.py:192
  1631.8 183.1 %reduce-scatter.33.cloned.1.call-done = f32[384,4096]{1,0:T(8,128)} async-done(((f32[1536,4096]{1,0:T(8,128)}), f32[384,4096]{1,0:T(8,128)}) %reduce-scatter.33.cloned.1.call-update) | async-done | bytes 6291472 | tf_op jit(solution)/shard_map/reduce_scatter | solution.py:195
  1814.9 183.1 %reduce-scatter.35.cloned.1.call-done = f32[1024,1536]{1,0:T(8,128)} async-done(((f32[4096,1536]{1,0:T(8,128)}), f32[1024,1536]{1,0:T(8,128)}) %reduce-scatter.35.cloned.1.call-update) | async-done | bytes 6291472 | tf_op jit(solution)/shard_map/reduce_scatter | solution.py:198
  1998.0 4.9 fusion.80
  2002.9 4.9 fusion.83
  2007.8 7.2 fusion.26
  2015.1 5.7 reduce-scatter.25.cloned.1.call-done
  2020.8 40.7 %psum.88 = f32[384,24]{0,1:T(8,128)} all-reduce(f32[384,24]{0,1:T(8,128)} %reduce-scatter.25.cloned.1.call-done), channel_id=1, replica_groups=mesh['ctx'=8,'fsdp'=4] {'ctx'}, use_global_device_ids=true, to_apply=%region_33.34 | all-reduce | flops 9216 | bytes 73728 | tf_op jit(solution)/shard_map/psum | solution.py:309
  2061.5 4.3 convolution_add_fusion.2
  2065.8 4.2 convolution_add_fusion.1
  2070.5 42.8 %all-reduce.2 = (f32[1536]{0:T(1024)}, f32[24]{0:T(128)}, f32[1536]{0:T(1024)}) all-reduce(f32[1536]{0:T(1024)S(1)} %get-tuple-element.623, f32[24]{0:T(128)S(1)} %get-tuple-element.709, f32[1536]{0:T(1024)S(1)} %copy-done.23), channel_id=1, replica_groups=mesh['ctx'=8,'fsdp'=4] {'ctx','fsdp'}, use_global_device_ids=true, to_apply=%region_25.26 | all-reduce | flops 3096 | bytes 24768 | tf_op jit(solution)/shard_map/psum | solution.py:323
  2114.5 822.6 %all-reduce.6.cloned.1.call-done = (f32[384,1536]{1,0:T(8,128)}, f32[384,1536]{1,0:T(8,128)}, f32[384,1536]{1,0:T(8,128)}, f32[384,1536]{1,0:T(8,128)}, f32[384,...) async-done(((f32[384,1536]{1,0:T(8,128)}, f32[384,1536]{1,0:T(8,128)}, f32[384,1536]{1,0:T(8,128)}, f32[384,1536]{1,0:T(8,128)}, ...) | async-done | bytes 30670864 | tf_op jit(solution)/shard_map/psum | solution.py:309
  2937.1 3.4 copy.121
  2948.2 3.2 copy.126
  2951.8 3.2 copy.127
  2956.3 2.7 copy.128
  (543 shorter events, 273.4 us)
Async XLA Ops:
  7.2 81.7 %copy-start.1 = (bf16[1,128,1536]{2,1,0:T(8,128)(2,1)S(1)}, bf16[1,128,1536]{2,1,0:T(8,128)(2,1)}, u32[]{:S(2)}) copy-start(bf16[1,128,1536]{2,1,0:T(8,128)(2,1)} %param.23) | copy-start | bytes 1179652
  7.2 42.6 %all-gather.13.cloned.1.call-start = ((), (), s32[]{:S(2)}) async-start(), calls=%async_computation.12 | async-start | bytes 5898240 | tf_op jit(solution)/shard_map/all_gather | solution.py:76
  7.9 80.9 %all-gather.19.cloned.1.call-start = ((), (), s32[]{:S(2)}) async-start(), calls=%async_computation.15 | async-start | bytes 5898240 | tf_op jit(solution)/shard_map/all_gather | solution.py:75
  8.7 153.4 %all-gather.17.cloned.1.call-start = ((), (), s32[]{:S(2)}) async-start(), calls=%async_computation.14 | async-start | bytes 5898240 | tf_op jit(solution)/shard_map/all_gather | solution.py:74
  9.4 183.3 %all-gather.15.cloned.1.call-start = ((), (), s32[]{:S(2)}) async-start(), calls=%async_computation.13 | async-start | bytes 3538944 | tf_op jit(solution)/shard_map/all_gather | solution.py:128
  53.9 200.6 %all-gather.21.cloned.1.call-start = ((), (), s32[]{:S(2)}) async-start(), calls=%async_computation.16 | async-start | bytes 3538944 | tf_op jit(solution)/shard_map/all_gather | solution.py:127
  92.8 312.1 %all-gather.23.cloned.1.call-start = ((), (), s32[]{:S(2)}) async-start(), calls=%async_computation.17 | async-start | bytes 5898240 | tf_op jit(solution)/shard_map/all_gather | solution.py:78
  93.4 316.2 %all-gather.25.cloned.1.call-start = ((), (), s32[]{:S(2)}) async-start(), calls=%async_computation.18 | async-start | bytes 5898240 | tf_op jit(solution)/shard_map/all_gather | solution.py:79
  94.1 2.2 copy-start.24
  94.1 8.1 copy-start.27
  94.1 9.2 copy-start.28
  94.1 320.6 %all-gather.27.cloned.1.call-start = ((), (), s32[]{:S(2)}) async-start(), calls=%async_computation.19 | async-start | bytes 15728640 | tf_op jit(solution)/shard_map/all_gather | solution.py:80
  94.9 66.0 %copy-start.26 = (bf16[1536]{0:T(1024)(128)(2,1)S(1)}, bf16[1536]{0:T(1024)(128)(2,1)}, u32[]{:S(2)}) copy-start(bf16[1536]{0:T(1024)(128)(2,1)} %param.33) | copy-start | bytes 9220
  94.9 66.6 %copy-start.16 = (s32[1,1024]{1,0:T(1,128)S(1)}, s32[1,1024]{1,0:T(1,128)}, u32[]{:S(2)}) copy-start(s32[1,1024]{1,0:T(1,128)} %param.24) | copy-start | bytes 12292
  94.9 403.5 %all-gather.29.cloned.1.call-start = ((), (), s32[]{:S(2)}) async-start(), calls=%async_computation.20 | async-start | bytes 15728640 | tf_op jit(solution)/shard_map/all_gather | solution.py:81
  95.6 486.4 %all-gather.31.cloned.1.call-start = ((), (), s32[]{:S(2)}) async-start(), calls=%async_computation.21 | async-start | bytes 15728640 | tf_op jit(solution)/shard_map/all_gather | solution.py:82
  96.2 766.4 %reduce-scatter.13.cloned.1.call-start = ((), (), s32[]{:S(2)}) async-start(), calls=%async_computation.22 | async-start | bytes 7077888 | tf_op jit(solution)/shard_map/reduce_scatter | solution.py:265
  101.6 0.6 copy-start.18
  402.0 7.5 copy-start.4
  409.5 3.4 copy-start.20
  422.5 159.6 %copy-start.14 = (bf16[1,128,1536]{2,1,0:T(8,128)(2,1)S(1)}, bf16[1,128,1536]{2,1,0:T(8,128)(2,1)}, u32[]{:S(2)}) copy-start(bf16[1,128,1536]{2,1,0:T(8,128)(2,1)} %param.37) | copy-start | bytes 1179652
  593.8 10.2 copy-start
  612.8 9.7 copy-start.2
  622.6 3.5 copy-start.21
  622.6 3.5 copy-start.22
  744.1 0.6 copy-start.17
  744.2 1.4 copy-start.6
  744.2 240.0 %reduce-scatter.15.cloned.1.call-start = ((), (), s32[]{:S(2)}) async-start(), calls=%async_computation.23 | async-start | bytes 7077888 | tf_op jit(solution)/shard_map/reduce_scatter | solution.py:266
  744.8 300.4 %reduce-scatter.17.cloned.1.call-start = ((), (), s32[]{:S(2)}) async-start(), calls=%async_computation.24 | async-start | bytes 110592 | tf_op jit(solution)/shard_map/reduce_scatter | solution.py:267
  745.5 379.6 %reduce-scatter.19.cloned.1.call-start = ((), (), s32[]{:S(2)}) async-start(), calls=%async_computation.25 | async-start | bytes 11796480 | tf_op jit(solution)/shard_map/reduce_scatter | solution.py:290
  750.8 455.3 %reduce-scatter.27.cloned.1.call-start = ((), (), s32[]{:S(2)}) async-start(), calls=%async_computation.29 | async-start | bytes 11796480 | tf_op jit(solution)/shard_map/reduce_scatter | solution.py:302
  755.8 1.1 copy-start.3
  755.9 531.1 %reduce-scatter.29.cloned.1.call-start = ((), (), s32[]{:S(2)}) async-start(), calls=%async_computation.30 | async-start | bytes 11796480 | tf_op jit(solution)/shard_map/reduce_scatter | solution.py:305
  762.9 604.9 %reduce-scatter.21.cloned.1.call-start = ((), (), s32[]{:S(2)}) async-start(), calls=%async_computation.26 | async-start | bytes 11796480 | tf_op jit(solution)/shard_map/reduce_scatter | solution.py:293
  868.9 579.9 %reduce-scatter.23.cloned.1.call-start = ((), (), s32[]{:S(2)}) async-start(), calls=%async_computation.27 | async-start | bytes 11796480 | tf_op jit(solution)/shard_map/reduce_scatter | solution.py:296
  990.4 641.4 %reduce-scatter.31.cloned.1.call-start = ((), (), s32[]{:S(2)}) async-start(), calls=%async_computation.31 | async-start | bytes 31457280 | tf_op jit(solution)/shard_map/reduce_scatter | solution.py:192
  1001.8 813.1 %reduce-scatter.33.cloned.1.call-start = ((), (), s32[]{:S(2)}) async-start(), calls=%async_computation.32 | async-start | bytes 31457280 | tf_op jit(solution)/shard_map/reduce_scatter | solution.py:195
  1013.2 1.0 copy-start.15
  1013.3 984.7 %reduce-scatter.35.cloned.1.call-start = ((), (), s32[]{:S(2)}) async-start(), calls=%async_computation.33 | async-start | bytes 31457280 | tf_op jit(solution)/shard_map/reduce_scatter | solution.py:198
  1025.7 40.8 %copy-start.25 = (f32[128,24]{0,1:T(8,128)S(1)}, f32[128,24]{0,1:T(8,128)}, u32[]{:S(2)}) copy-start(f32[128,24]{0,1:T(8,128)} %get-tuple-element.728) | copy-start | bytes 36868
  1025.8 995.0 %reduce-scatter.25.cloned.1.call-start = ((), (), s32[]{:S(2)}) async-start(), calls=%async_computation.28 | async-start | bytes 184320 | tf_op jit(solution)/shard_map/reduce_scatter | solution.py:299
  1067.7 1869.4 %all-reduce.6.cloned.1.call-start = ((), (), s32[]{:S(2)}) async-start(), calls=%async_computation.34 | async-start | bytes 61341696 | tf_op jit(solution)/shard_map/psum | solution.py:309
  1998.0 9.8 copy-start.5
  2007.8 53.7 %copy-start.7 = (f32[128,1536]{0,1:T(8,128)S(1)}, f32[128,1536]{0,1:T(8,128)}, u32[]{:S(2)}) copy-start(f32[128,1536]{0,1:T(8,128)} %reduce-scatter.13.cloned.1.call-done) | copy-start | bytes 2359300
  2015.1 50.7 %copy-start.8 = (f32[128,1536]{0,1:T(8,128)S(1)}, f32[128,1536]{0,1:T(8,128)}, u32[]{:S(2)}) copy-start(f32[128,1536]{0,1:T(8,128)} %reduce-scatter.15.cloned.1.call-done) | copy-start | bytes 2359300
  2065.8 4.2 copy-start.9
  2065.8 4.2 copy-start.19
  2065.8 4.7 copy-start.23
  2937.1 3.4 copy-start.13
  2937.1 4.8 copy-start.12
  2940.5 2.9 copy-start.11
  2941.9 3.4 copy-start.10
  2941.9 5.7 slice-start.4
  2943.3 4.8 slice-start.5
  2945.3 6.1 slice-start.2
  2948.2 3.7 slice-start.3
  2948.2 6.9 slice-start
  2951.8 4.5 slice-start.1
Sparse Core Ops, SparseCore 0:
  9.6 40.1 all-gather.12
  51.3 37.4 all-gather.18
  90.4 37.4 all-gather.16
  130.5 62.1 all-gather.14
  195.3 59.0 all-gather.20
  255.9 36.0 all-gather.22
  293.5 37.4 all-gather.24
  332.6 82.1 all-gather.26
  416.3 82.0 all-gather.28
  499.9 82.1 all-gather.30
  744.3 118.2 reduce-scatter.12
  866.6 117.4 reduce-scatter.14
  988.0 57.1 reduce-scatter.16
  1047.6 77.4 reduce-scatter.18
  1127.6 78.4 reduce-scatter.26
  1208.5 78.4 reduce-scatter.28
  1289.4 78.4 reduce-scatter.20
  1370.3 78.4 reduce-scatter.22
  1451.3 180.4 reduce-scatter.30
  1634.4 180.4 reduce-scatter.32
  1817.5 180.4 reduce-scatter.34
  2001.1 19.6 reduce-scatter.24
  2027.5 909.4 all-reduce.5
where the time goes:
time: 2980 us; the launch traced here: 2970 us
  waiting for transfers between devices  2310 us (78%)
  matrix products  216 us (7%)
  local copies, waits for them, and re-layouts  208 us (7%)
  blocking collectives  162 us (5%)
  other arithmetic  34.6 us (1%)
    psum x1, waiting for transfers between devices, shards(): lax.psum((ffn_parts[0], ffn_parts[1], ffn_parts[2], attn_parts[0], attn_p...  823 us
    reduce_scatter x1, waiting for transfers between devices, shards(): lax.psum_scatter(weight_grad(normed_two, grad_up_low), 'fsdp', scatter_di...  183 us
    reduce_scatter x1, waiting for transfers between devices, shards(): lax.psum_scatter(weight_grad(hidden, grad_out_low), 'fsdp', scatter_dimen...  183 us
    reduce_scatter x1, waiting for transfers between devices, shards(): lax.psum_scatter(weight_grad(normed_two, grad_gate_low), 'fsdp', scatter_...  183 us
    reduce_scatter x1, waiting for transfers between devices, shards(): lax.psum_scatter(grad_values, 'ctx', scatter_dimension=0, tiled=True)  115 us
    reduce_scatter x1, waiting for transfers between devices, shards(): lax.psum_scatter(grad_keys, 'ctx', scatter_dimension=0, tiled=True)  99.6 us
    reduce_scatter x1, waiting for transfers between devices, shards(): lax.psum_scatter(weight_grad(gated_out, grad_branch_low), 'fsdp', scatter...  80.9 us
    reduce_scatter x1, waiting for transfers between devices, shards(): lax.psum_scatter(weight_grad(normed, grad_value_low), 'fsdp', scatter_dim...  80.9 us
  transfers between devices with their start and end apart: 23, of which 20 were waited for; matrix products, arithmetic and copies ran while one was open for 9% of the time, Pallas kernels for 0%

commit v1 on v0

--- a/solution.py
+++ b/solution.py
@@ -6,6 +6,32 @@
 
 EPSILON = 1e-06
 NEGATIVE = -1e30
+
+
+def _define_column(matrix, row_dim):
+    matrix = jnp.moveaxis(matrix, 0, row_dim)
+    piece_now = matrix.shape
+    return matrix.reshape(
+        *piece_now[:row_dim], piece_now[row_dim] * piece_now[row_dim + 1], *piece_now[row_dim + 2 :]
+    )
+
+
+def balance_the_heaps(xin, axis_tag, axis_k):
+    n = lax.axis_size(axis_tag)
+    shelf = [(pp, (pp + 1) % n) for pp in range(n)]
+    sheets = [(idx, ii) for ii, idx in shelf]
+    formed, extra = ([], [])
+    for hop_no in tuple(range(n - 1)):
+        if hop_no % 2 == 0:
+            formed.append(lax.ppermute(formed[-1] if formed else xin, axis_tag, shelf))
+        else:
+            extra.append(lax.ppermute(extra[-1] if extra else xin, axis_tag, sheets))
+    z = jnp.stack([*formed[::-1], xin, *extra])
+    current_value = len(formed)
+    latest = lax.axis_index(axis_tag)
+    tile_out = latest - current_value
+    z = z[(jnp.arange(n) - tile_out) % n]
+    return _define_column(z, axis_k)
 
 
 def entering(value, axis, join, neutral, backward):
@@ -78,7 +104,7 @@
         lax.all_gather(w_outgate, "fsdp", axis=0, tiled=True),
         lax.all_gather(w_out, "fsdp", axis=0, tiled=True),
         lax.all_gather(w_gate, "fsdp", axis=0, tiled=True),
-        lax.all_gather(w_up, "fsdp", axis=0, tiled=True),
+        balance_the_heaps(w_up, "fsdp", 0),
         lax.all_gather(w_down, "fsdp", axis=0, tiled=True),
     )
     (

time: 2980 us -> 2920 us (0.980)
  waiting for transfers between devices: 2310 us -> 2160 us
  blocking collectives: 162 us -> 196 us
    ppermute x0 -> x3, waiting for transfers between devices: none -> 93.5 us  [the longest x2 93.5 us: balance_the_heaps(): formed.append(lax.ppermute(formed[-1] if formed else xin, axis_tag, shelf))]
    all_gather x1 -> x0, waiting for transfers between devices: 76 us -> none  [shards(): lax.all_gather(w_up, 'fsdp', axis=0, tiled=True)]
    all_gather x1, waiting for transfers between devices: 75.9 us -> 0.01 us  [shards(): lax.all_gather(w_down, 'fsdp', axis=0, tiled=True)]
    all_gather x1, waiting for transfers between devices: 58.5 us -> 0.02 us  [shards(): lax.all_gather(key_own, 'ctx', axis=0, tiled=True)]
    all_gather x1, blocking collectives: 5.3 us -> 37.9 us  [shards(): lax.all_gather(w_forget, 'fsdp', axis=0, tiled=True)]
  transfers between devices with their start and end apart: 23 -> 25, of which waited for: 20 -> 16; matrix products, arithmetic and copies ran while one was open for 9% -> 11% of each run, Pallas kernels for 0% -> 0%
where the time goes in v1:
time: 2920 us; the launch traced here: 2910 us
  waiting for transfers between devices  2160 us (74%)
  local copies, waits for them, and re-layouts  234 us (8%)
  matrix products  213 us (7%)
  blocking collectives  196 us (7%)
  other arithmetic  64.1 us (2%)
    psum x1, waiting for transfers between devices, shards(): lax.psum((ffn_parts[0], ffn_parts[1], ffn_parts[2], attn_parts[0], attn_p...  823 us
    reduce_scatter x1, waiting for transfers between devices, shards(): lax.psum_scatter(weight_grad(normed_two, grad_up_low), 'fsdp', scatter_di...  183 us
    reduce_scatter x1, waiting for transfers between devices, shards(): lax.psum_scatter(weight_grad(normed_two, grad_gate_low), 'fsdp', scatter_...  183 us
    reduce_scatter x1, waiting for transfers between devices, shards(): lax.psum_scatter(weight_grad(hidden, grad_out_low), 'fsdp', scatter_dimen...  183 us
    reduce_scatter x1, waiting for transfers between devices, shards(): lax.psum_scatter(grad_values, 'ctx', scatter_dimension=0, tiled=True)  115 us
    reduce_scatter x1, waiting for transfers between devices, shards(): lax.psum_scatter(grad_keys, 'ctx', scatter_dimension=0, tiled=True)  97.1 us
    ppermute x2, waiting for transfers between devices, balance_the_heaps(): formed.append(lax.ppermute(formed[-1] if formed else xin, axis_tag, shelf))  93.5 us
    reduce_scatter x1, waiting for transfers between devices, shards(): lax.psum_scatter(weight_grad(normed, grad_key_low), 'fsdp', scatter_dimen...  80.8 us
  transfers between devices with their start and end apart: 25, of which 16 were waited for; matrix products, arithmetic and copies ran while one was open for 11% of the time, Pallas kernels for 0%

profile of v1, /device:TPU:0, one launch (start us, length us, event | category | flops | bytes accessed | tf_op | source)
XLA Modules:
  0.0 2905.3 jit_solution(17461927499365163301)
XLA Ops:
  11.3 38.5 %all-gather.12.cloned.1.call-done = bf16[1536,1536]{1,0:T(8,128)(2,1)} async-done(((bf16[384,1536]{1,0:T(8,128)(2,1)}), bf16[1536,1536]{1,0:T(8,128)(2,1)}) %all-gather.12.cloned.1.call-update) | async-done | bytes 4718608 | tf_op jit(solution)/shard_map/all_gather | solution.py:102
  49.8 4.0 convolution_convert_fusion.2
  53.9 34.9 %all-gather.18.cloned.1.call-done = bf16[1536,1536]{1,0:T(8,128)(2,1)} async-done(((bf16[384,1536]{1,0:T(8,128)(2,1)}), bf16[1536,1536]{1,0:T(8,128)(2,1)}) %all-gather.18.cloned.1.call-update) | async-done | bytes 4718608 | tf_op jit(solution)/shard_map/all_gather | solution.py:101
  88.8 3.9 convolution_convert_fusion
  96.7 93.5 %collective-permute-done = bf16[384,4096]{1,0:T(8,128)(2,1)} collective-permute-done((bf16[384,4096]{1,0:T(8,128)(2,1)S(1)}, bf16[384,4096]{1,0:T(8,128)(2,1)}, u32[]{:S(2)}, u32[]{:S(2)}) %collective-permute-start) | collective-permute-done | bytes 3145760 | tf_op jit(solution)/shard_map/ppermute | solution.py:26
  190.3 37.9 %all_gather.48 = bf16[1536,24]{0,1:T(8,128)(2,1)S(1)} all-gather(bf16[384,24]{0,1:T(8,128)(2,1)} %param.29), channel_id=1, replica_groups=mesh['ctx'=8,'fsdp'=4] {'fsdp'}, dimensions={0}, use_global_device_ids=true | all-gather | bytes 92160 | tf_op jit(solution)/shard_map/all_gather | solution.py:103
  228.8 2.2 fusion.61
  236.2 22.2 all-reduce
  261.4 8.5 while.65
  272.9 33.7 %all_gather.50 = f32[1024,24]{1,0:T(8,128)} all-gather(f32[128,24]{1,0:T(8,128)} %broadcast_add_fusion), channel_id=1, replica_groups=mesh['ctx'=8,'fsdp'=4] {'ctx'}, dimensions={0}, use_global_device_ids=true | all-gather | bytes 110592 | tf_op jit(solution)/shard_map/all_gather | solution.py:151
  311.4 5.6 pad_maximum_fusion
  317.1 5.1 fusion.78
  322.2 7.0 gather_fusion.1
  329.2 6.6 gather_fusion
  335.8 10.6 pad_maximum_fusion.1
  346.4 3.2 convolution_convert_fusion.1
  350.5 3.2 copy.45
  353.7 4.6 copy.47
  358.9 142.4 %while.63 = (s32[]{:T(128)}, f32[12,128,128]{1,2,0:T(8,128)}, f32[12,2,128]{2,1,0:T(2,128)}, s32[12]{0:T(128)}, bf16[1024,1536]{0,1:T(8,128)(2,1)S(1)}, /*index=...) while((s32[]{:T(128)}, f32[12,128,128]{1,2,0:T(8,128)}, ...), condition=%wide.region_8.9_spmd.clone, body=%wide.region_5.8_spmd.clone.sunk | while | flops 70123272 | bytes 5316909 | solution.py:192
  501.3 2.9 copy.50
  504.1 4.5 multiply_convert_fusion.6
  508.6 3.4 multiply_reduce_fusion.3
  512.2 7.8 fusion.81
  520.0 7.9 fusion.80
  527.9 11.0 multiply_convert_fusion.1
  538.9 9.6 fusion.82
  548.6 9.9 multiply_reduce_fusion.1
  558.8 2.4 multiply_convert_fusion.4
  562.1 3.5 broadcast.170
  565.6 3.5 broadcast.170.clone
  569.1 117.9 %while.64 = (s32[]{:T(128)}, bf16[128,1536]{0,1:T(8,128)(2,1)}, f32[1024,1536]{0,1:T(8,128)}, f32[1024,1536]{0,1:T(8,128)}, f32[128,24]{0,1:T(8,128)S(1)}, /*ind...) while((s32[]{:T(128)}, bf16[128,1536]{0,1:T(8,128)(2,1)}, ...), condition=%wide.region_15.16_spmd.clone, body=%wide.region_11.15_spmd.clone.sunk | while | flops 171998720 | bytes 13599061 | solution.py:287
  688.4 5.2 fusion.52
  693.7 5.0 fusion.64
  699.9 4.9 fusion.56
  705.0 97.1 %reduce-scatter.13.cloned.1.call-done = f32[128,1536]{0,1:T(8,128)} async-done(((f32[1024,1536]{0,1:T(8,128)}), f32[128,1536]{0,1:T(8,128)}) %reduce-scatter.13.cloned.1.call-update) | async-done | bytes 786448 | tf_op jit(solution)/shard_map/reduce_scatter | solution.py:291
  802.1 6.2 fusion.49
  808.6 115.2 %reduce-scatter.15.cloned.1.call-done = f32[128,1536]{0,1:T(8,128)} async-done(((f32[1024,1536]{0,1:T(8,128)}), f32[128,1536]{0,1:T(8,128)}) %reduce-scatter.15.cloned.1.call-update) | async-done | bytes 786448 | tf_op jit(solution)/shard_map/reduce_scatter | solution.py:292
  923.8 6.2 fusion.46
  930.1 11.4 fusion.84
  941.5 11.4 fusion.85
  954.2 10.2 fusion.42
  964.5 20.2 reduce-scatter.17.cloned.1.call-done
  986.2 19.5 all-reduce.1
  1007.7 57.0 %reduce-scatter.19.cloned.1.call-done = f32[384,1536]{1,0:T(8,128)} async-done(((f32[1536,1536]{1,0:T(8,128)}), f32[384,1536]{1,0:T(8,128)}) %reduce-scatter.19.cloned.1.call-update) | async-done | bytes 2359312 | tf_op jit(solution)/shard_map/reduce_scatter | solution.py:316
  1064.8 80.8 %reduce-scatter.27.cloned.1.call-done = f32[384,1536]{1,0:T(8,128)} async-done(((f32[1536,1536]{1,0:T(8,128)}), f32[384,1536]{1,0:T(8,128)}) %reduce-scatter.27.cloned.1.call-update) | async-done | bytes 2359312 | tf_op jit(solution)/shard_map/reduce_scatter | solution.py:328
  1145.6 80.8 %reduce-scatter.29.cloned.1.call-done = f32[384,1536]{1,0:T(8,128)} async-done(((f32[1536,1536]{1,0:T(8,128)}), f32[384,1536]{1,0:T(8,128)}) %reduce-scatter.29.cloned.1.call-update) | async-done | bytes 2359312 | tf_op jit(solution)/shard_map/reduce_scatter | solution.py:331
  1226.4 80.8 %reduce-scatter.21.cloned.1.call-done = f32[384,1536]{1,0:T(8,128)} async-done(((f32[1536,1536]{1,0:T(8,128)}), f32[384,1536]{1,0:T(8,128)}) %reduce-scatter.21.cloned.1.call-update) | async-done | bytes 2359312 | tf_op jit(solution)/shard_map/reduce_scatter | solution.py:319
  1307.2 80.8 %reduce-scatter.23.cloned.1.call-done = f32[384,1536]{1,0:T(8,128)} async-done(((f32[1536,1536]{1,0:T(8,128)}), f32[384,1536]{1,0:T(8,128)}) %reduce-scatter.23.cloned.1.call-update) | async-done | bytes 2359312 | tf_op jit(solution)/shard_map/reduce_scatter | solution.py:322
  1388.1 182.9 %reduce-scatter.31.cloned.1.call-done = f32[384,4096]{1,0:T(8,128)} async-done(((f32[1536,4096]{1,0:T(8,128)}), f32[384,4096]{1,0:T(8,128)}) %reduce-scatter.31.cloned.1.call-update) | async-done | bytes 6291472 | tf_op jit(solution)/shard_map/reduce_scatter | solution.py:218
  1571.0 183.2 %reduce-scatter.33.cloned.1.call-done = f32[384,4096]{1,0:T(8,128)} async-done(((f32[1536,4096]{1,0:T(8,128)}), f32[384,4096]{1,0:T(8,128)}) %reduce-scatter.33.cloned.1.call-update) | async-done | bytes 6291472 | tf_op jit(solution)/shard_map/reduce_scatter | solution.py:221
  1754.2 182.9 %reduce-scatter.35.cloned.1.call-done = f32[1024,1536]{1,0:T(8,128)} async-done(((f32[4096,1536]{1,0:T(8,128)}), f32[1024,1536]{1,0:T(8,128)}) %reduce-scatter.35.cloned.1.call-update) | async-done | bytes 6291472 | tf_op jit(solution)/shard_map/reduce_scatter | solution.py:224
  1938.1 4.9 fusion.83
  1943.0 4.9 fusion.86
  1947.9 7.1 fusion.26
  1955.1 4.9 reduce-scatter.25.cloned.1.call-done
  1960.0 40.7 %psum.88 = f32[384,24]{0,1:T(8,128)} all-reduce(f32[384,24]{0,1:T(8,128)} %reduce-scatter.25.cloned.1.call-done), channel_id=1, replica_groups=mesh['ctx'=8,'fsdp'=4] {'ctx'}, use_global_device_ids=true, to_apply=%region_33.34 | all-reduce | flops 9216 | bytes 73728 | tf_op jit(solution)/shard_map/psum | solution.py:335
  2000.6 4.5 convolution_add_fusion.2
  2005.3 4.1 convolution_add_fusion.1
  2009.9 42.6 %all-reduce.2 = (f32[1536]{0:T(1024)}, f32[24]{0:T(128)}, f32[1536]{0:T(1024)}) all-reduce(f32[1536]{0:T(1024)S(1)} %get-tuple-element.623, f32[24]{0:T(128)S(1)} %copy-done.36, f32[1536]{0:T(1024)S(1)} %copy-done.32), channel_id=1, replica_groups=mesh['ctx'=8,'fsdp'=4] {'ctx','fsdp'}, use_global_device_ids=true, to_apply=%region_25.26 | all-reduce | flops 3096 | bytes 24768 | tf_op jit(solution)/shard_map/psum | solution.py:349
  2053.7 822.6 %all-reduce.6.cloned.1.call-done = (f32[384,1536]{1,0:T(8,128)}, f32[384,1536]{1,0:T(8,128)}, f32[384,1536]{1,0:T(8,128)}, f32[384,1536]{1,0:T(8,128)}, f32[384,...) async-done(((f32[384,1536]{1,0:T(8,128)}, f32[384,1536]{1,0:T(8,128)}, f32[384,1536]{1,0:T(8,128)}, f32[384,1536]{1,0:T(8,128)}, ...) | async-done | bytes 30670864 | tf_op jit(solution)/shard_map/psum | solution.py:335
  2876.3 3.4 copy.121
  2887.3 3.2 copy.126
  2891.0 3.2 copy.127
  2895.5 2.7 copy.128
  (574 shorter events, 298.5 us)
Async XLA Ops:
  7.2 81.7 %copy-start = (bf16[1,128,1536]{2,1,0:T(8,128)(2,1)S(1)}, bf16[1,128,1536]{2,1,0:T(8,128)(2,1)}, u32[]{:S(2)}) copy-start(bf16[1,128,1536]{2,1,0:T(8,128)(2,1)} %param.23) | copy-start | bytes 1179652
  7.2 42.6 %all-gather.12.cloned.1.call-start = ((), (), s32[]{:S(2)}) async-start(), calls=%async_computation.12 | async-start | bytes 5898240 | tf_op jit(solution)/shard_map/all_gather | solution.py:102
  7.9 80.9 %all-gather.18.cloned.1.call-start = ((), (), s32[]{:S(2)}) async-start(), calls=%async_computation.15 | async-start | bytes 5898240 | tf_op jit(solution)/shard_map/all_gather | solution.py:101
  8.7 337.7 %all-gather.16.cloned.1.call-start = ((), (), s32[]{:S(2)}) async-start(), calls=%async_computation.14 | async-start | bytes 5898240 | tf_op jit(solution)/shard_map/all_gather | solution.py:100
  9.4 341.1 %all-gather.14.cloned.1.call-start = ((), (), s32[]{:S(2)}) async-start(), calls=%async_computation.13 | async-start | bytes 3538944 | tf_op jit(solution)/shard_map/all_gather | solution.py:154
  53.9 41.1 %copy-start.12 = (bf16[384,4096]{1,0:T(8,128)(2,1)S(1)}, bf16[384,4096]{1,0:T(8,128)(2,1)}, u32[]{:S(2)}) copy-start(bf16[384,4096]{1,0:T(8,128)(2,1)} %param.35) | copy-start | bytes 9437188
  53.9 299.9 %all-gather.20.cloned.1.call-start = ((), (), s32[]{:S(2)}) async-start(), calls=%async_computation.16 | async-start | bytes 3538944 | tf_op jit(solution)/shard_map/all_gather | solution.py:153
  92.8 411.3 %all-gather.22.cloned.1.call-start = ((), (), s32[]{:S(2)}) async-start(), calls=%async_computation.17 | async-start | bytes 5898240 | tf_op jit(solution)/shard_map/all_gather | solution.py:104
  93.4 415.3 %all-gather.24.cloned.1.call-start = ((), (), s32[]{:S(2)}) async-start(), calls=%async_computation.18 | async-start | bytes 5898240 | tf_op jit(solution)/shard_map/all_gather | solution.py:105
  94.1 216.1 %copy-start.23 = (s32[1,1024]{1,0:T(1,128)S(1)}, s32[1,1024]{1,0:T(1,128)}, u32[]{:S(2)}) copy-start(s32[1,1024]{1,0:T(1,128)} %param.24) | copy-start | bytes 12292
  94.1 425.9 %all-gather.26.cloned.1.call-start = ((), (), s32[]{:S(2)}) async-start(), calls=%async_computation.19 | async-start | bytes 15728640 | tf_op jit(solution)/shard_map/all_gather | solution.py:106
  94.9 433.0 %all-gather.28.cloned.1.call-start = ((), (), s32[]{:S(2)}) async-start(), calls=%async_computation.20 | async-start | bytes 15728640 | tf_op jit(solution)/shard_map/all_gather | solution.py:108
  94.9 95.3 %collective-permute-start = (bf16[384,4096]{1,0:T(8,128)(2,1)S(1)}, bf16[384,4096]{1,0:T(8,128)(2,1)}, u32[]{:S(2)}, u32[]{:S(2)}) collective-permute-start(bf16[384,4096]{1,0:T(8,128)(2,1)S(1)} %copy-done.12), channel_id=1, source_target_pairs={{0,1},{1,2},{2,3},{3,0},{4,5},{5,6},{6,7},{7,4},{8,9},{9,10},{10,1... | collective-permute-start | bytes 9437192 | tf_op jit(solution)/shard_map/ppermute | solution.py:26
  95.2 216.2 %collective-permute-start.2 = (bf16[384,4096]{1,0:T(8,128)(2,1)S(1)}, bf16[384,4096]{1,0:T(8,128)(2,1)}, u32[]{:S(2)}, u32[]{:S(2)}) collective-permute-start(bf16[384,4096]{1,0:T(8,128)(2,1)S(1)} %copy-done.12), channel_id=1, source_target_pairs={{1,0},{2,1},{3,2},{0,3},{5,4},{6,5},{7,6},{4,7},{9,8},{10,9},{11,1... | collective-permute-start | bytes 9437192 | tf_op jit(solution)/shard_map/ppermute | solution.py:28
  190.2 121.2 %collective-permute-start.1 = (bf16[384,4096]{1,0:T(8,128)(2,1)}, bf16[384,4096]{1,0:T(8,128)(2,1)}, u32[]{:S(2)}, u32[]{:S(2)}) collective-permute-start(bf16[384,4096]{1,0:T(8,128)(2,1)} %collective-permute-done), channel_id=1, source_target_pairs={{0,1},{1,2},{2,3},{3,0},{4,5},{5,6},{6,7},{7,4},{8,9},{9,10},{10,1... | collective-permute-start | bytes 9437192 | tf_op jit(solution)/shard_map/ppermute | solution.py:26
  190.2 611.9 %reduce-scatter.13.cloned.1.call-start = ((), (), s32[]{:S(2)}) async-start(), calls=%async_computation.21 | async-start | bytes 7077888 | tf_op jit(solution)/shard_map/reduce_scatter | solution.py:291
  501.2 7.4 copy-start.3
  508.6 3.4 copy-start.27
  520.0 7.9 copy-start.20
  538.9 9.6 copy-start.6
  538.9 9.6 copy-start.5
  548.5 10.2 slice-start
  548.5 10.2 slice-start.1
  548.5 10.2 copy-start.14
  548.6 10.2 copy-start.22
  558.7 6.8 copy-start.1
  561.2 132.4 %copy-start.7 = (bf16[128,1536]{1,0:T(8,128)(2,1)}, bf16[128,1536]{1,0:T(8,128)(2,1)S(1)}, u32[]{:S(2)}) copy-start(bf16[128,1536]{1,0:T(8,128)(2,1)S(1)} %get-tuple-element.727) | copy-start | bytes 1179652
  565.6 3.5 copy-start.28
  565.6 3.5 copy-start.29
  687.0 1.4 copy-start.9
  687.0 236.8 %reduce-scatter.15.cloned.1.call-start = ((), (), s32[]{:S(2)}) async-start(), calls=%async_computation.22 | async-start | bytes 7077888 | tf_op jit(solution)/shard_map/reduce_scatter | solution.py:292
  687.8 296.9 %reduce-scatter.17.cloned.1.call-start = ((), (), s32[]{:S(2)}) async-start(), calls=%async_computation.23 | async-start | bytes 110592 | tf_op jit(solution)/shard_map/reduce_scatter | solution.py:293
  688.4 376.4 %reduce-scatter.19.cloned.1.call-start = ((), (), s32[]{:S(2)}) async-start(), calls=%async_computation.24 | async-start | bytes 11796480 | tf_op jit(solution)/shard_map/reduce_scatter | solution.py:316
  693.6 452.0 %reduce-scatter.27.cloned.1.call-start = ((), (), s32[]{:S(2)}) async-start(), calls=%async_computation.28 | async-start | bytes 11796480 | tf_op jit(solution)/shard_map/reduce_scatter | solution.py:328
  698.7 1.2 copy-start.19
  698.7 527.7 %reduce-scatter.29.cloned.1.call-start = ((), (), s32[]{:S(2)}) async-start(), calls=%async_computation.29 | async-start | bytes 11796480 | tf_op jit(solution)/shard_map/reduce_scatter | solution.py:331
  704.9 602.3 %reduce-scatter.21.cloned.1.call-start = ((), (), s32[]{:S(2)}) async-start(), calls=%async_computation.25 | async-start | bytes 11796480 | tf_op jit(solution)/shard_map/reduce_scatter | solution.py:319
  808.3 579.7 %reduce-scatter.23.cloned.1.call-start = ((), (), s32[]{:S(2)}) async-start(), calls=%async_computation.26 | async-start | bytes 11796480 | tf_op jit(solution)/shard_map/reduce_scatter | solution.py:322
  930.0 641.0 %reduce-scatter.31.cloned.1.call-start = ((), (), s32[]{:S(2)}) async-start(), calls=%async_computation.30 | async-start | bytes 31457280 | tf_op jit(solution)/shard_map/reduce_scatter | solution.py:218
  941.5 812.8 %reduce-scatter.33.cloned.1.call-start = ((), (), s32[]{:S(2)}) async-start(), calls=%async_computation.31 | async-start | bytes 31457280 | tf_op jit(solution)/shard_map/reduce_scatter | solution.py:221
  952.9 1.3 copy-start.21
  952.9 984.2 %reduce-scatter.35.cloned.1.call-start = ((), (), s32[]{:S(2)}) async-start(), calls=%async_computation.32 | async-start | bytes 31457280 | tf_op jit(solution)/shard_map/reduce_scatter | solution.py:224
  964.4 20.3 copy-start.31
  964.4 41.6 %copy-start.35 = (f32[128,24]{0,1:T(8,128)S(1)}, f32[128,24]{0,1:T(8,128)}, u32[]{:S(2)}) copy-start(f32[128,24]{0,1:T(8,128)} %get-tuple-element.730) | copy-start | bytes 36868
  964.4 995.5 %reduce-scatter.25.cloned.1.call-start = ((), (), s32[]{:S(2)}) async-start(), calls=%async_computation.27 | async-start | bytes 184320 | tf_op jit(solution)/shard_map/reduce_scatter | solution.py:325
  1006.7 930.4 %copy-start.33 = (bf16[128,24]{0,1:T(8,128)(2,1)}, bf16[128,24]{0,1:T(8,128)(2,1)S(1)}, u32[]{:S(2)}) copy-start(bf16[128,24]{0,1:T(8,128)(2,1)S(1)} %get-tuple-element.710) | copy-start | bytes 18436
  1007.7 1868.6 %all-reduce.6.cloned.1.call-start = ((), (), s32[]{:S(2)}) async-start(), calls=%async_computation.33 | async-start | bytes 61341696 | tf_op jit(solution)/shard_map/psum | solution.py:335
  1938.1 4.9 copy-start.10
  1955.1 50.1 %copy-start.11 = (f32[128,1536]{0,1:T(8,128)S(1)}, f32[128,1536]{0,1:T(8,128)}, u32[]{:S(2)}) copy-start(f32[128,1536]{0,1:T(8,128)} %reduce-scatter.15.cloned.1.call-done) | copy-start | bytes 2359300
  2005.2 4.2 copy-start.13
  2005.2 4.2 copy-start.26
  2005.2 4.2 copy-start.34
  2005.2 4.7 copy-start.32
  2005.2 4.7 copy-start.36
  2876.3 3.4 copy-start.18
  2876.3 4.8 copy-start.17
  2879.6 2.9 copy-start.16
  2881.1 3.4 copy-start.15
  2881.1 5.7 slice-start.6
  2882.5 4.8 slice-start.7
  2884.4 6.1 slice-start.4
  2887.3 3.7 slice-start.5
  2887.3 6.9 slice-start.2
  2891.0 4.5 slice-start.3
  (6 other events, 5.6 us)
Sparse Core Ops, SparseCore 0:
  9.6 40.1 all-gather.11
  51.3 37.4 all-gather.17
  90.4 62.8 all-gather.15
  155.9 60.4 all-gather.13
  219.0 60.3 all-gather.19
  280.8 36.8 all-gather.21
  319.2 37.4 all-gather.23
  358.3 82.1 all-gather.25
  442.0 82.0 all-gather.27
  687.1 114.8 reduce-scatter.12
  806.3 117.5 reduce-scatter.14
  927.5 57.1 reduce-scatter.16
  987.3 77.4 reduce-scatter.18
  1067.2 78.3 reduce-scatter.26
  1148.0 78.3 reduce-scatter.28
  1228.9 78.3 reduce-scatter.20
  1309.7 78.3 reduce-scatter.22
  1390.5 180.4 reduce-scatter.30
  1573.8 180.4 reduce-scatter.32
  1756.7 180.4 reduce-scatter.34
  1940.3 19.6 reduce-scatter.24
  1966.7 909.5 all-reduce.5
